TPU v7x, 32 devices: a whole 2x2x4 slice. The times are simulated.
32 devices in a mesh: parts: 2 (over x), leaf: 16 (over z, y, core).
Axes of the slice: x: 2, y: 2, z: 4, core: 2. Of those that a mesh axis runs over, the one named last changes fastest.
Arguments:
- right_sides: bfloat16 [128, 16384], P('parts', 'leaf'), parts along dimension 0, may hold values from -6 to 6
- near_list: int32 [32, 3], P(('parts', 'leaf')), parts along dimension 0, may hold values from 0 to 15, as said below
- near_blocks: bfloat16 [32, 3, 1024, 1024], P(('parts', 'leaf')), parts along dimension 0, may hold values from -0.02734375 to 0.02734375
- inverse_list: int32 [32, 2], P(('parts', 'leaf')), parts along dimension 0, may hold values from 0 to 15, as said below
- inverse_blocks: bfloat16 [32, 2, 1024, 1024], P(('parts', 'leaf')), parts along dimension 0, may hold values from -0.03125 to 0.03125
- leaf_bases: bfloat16 [32, 1024, 128], P(('parts', 'leaf')), parts along dimension 0, may hold values from -0.1875 to 0.1875
- transfers: bfloat16 [2, 2, 128, 128], replicated, may hold values from -0.375 to 0.375
- couple_list: int32 [32, 3, 4], P(('parts', 'leaf')), parts along dimension 0, may hold values from 0 to 15, as said below
- couple_blocks: bfloat16 [32, 3, 4, 128, 128], P(('parts', 'leaf')), parts along dimension 0, may hold values from -0.125 to 0.125
Outputs:
- solution: float32 [128, 16384], P('parts', 'leaf'), parts along dimension 0
- residual: float32 [128, 16384], P('parts', 'leaf'), parts along dimension 0
There are 2 independent parts, one for each index of `parts`. A program takes and returns all parts, laid end to end along the dimension named above; an argument that names none is the same for every part. Nothing has to cross between parts.
Inputs may be any that keep to these rules, and one draw needn't show every extreme that they name: `near_list`: entry [i, s] lies within 2 of i. `inverse_list`: entry [i, s] lies within 2 of i. `couple_list`: entry [i, l, k] names a cluster of level l, below 16 // 2 ** l.
All inputs are finite; a program needn't handle non-finite values.
Results may differ from a plain program's by a relative error of at most 0.014.
Values may be sent and summed in bfloat16 or wider, within the bound.
No kernel may reach another device: no remote copies, remote signals or barrier semaphores. Data moves between devices by JAX's collectives and lax.ppermute only.
A program may use at most 64 MiB of HBM per device.

v0:
```python
import jax
import jax.numpy as jnp
from jax import lax
from jax.sharding import PartitionSpec as P

REACH = 2


exact_mode = lax.Precision.HIGHEST


def from_behind(value, axis, steps):
    count = lax.axis_size(axis)
    first, last = (max(0, -steps), min(count, count - steps))
    return lax.ppermute(value, axis, [(source, source + steps) for source in range(first, last)])


def partner(value, axis, apart):
    mask = 2**apart
    pairs = [(source, source ^ mask) for source in range(lax.axis_size(axis))]
    return lax.ppermute(value, axis, pairs)


def neighbourhood(half_vector):
    received = {0: half_vector}
    for offset in range(-REACH, REACH + 1):
        if offset != 0:
            received[offset] = from_behind(half_vector, "leaf", -offset)
    return jnp.stack([received[offset] for offset in range(-REACH, REACH + 1)])


def apply_slots(window, relative, blocks):
    running = jnp.zeros(window.shape[1:], jnp.float32)
    for slot_index in range(blocks.shape[0]):
        chosen = lax.dynamic_index_in_dim(window, relative[slot_index], 0, keepdims=False)
        running = running + jnp.dot(chosen, blocks[slot_index], preferred_element_type=jnp.float32)
    return running


def select_map(child_maps, position):
    return lax.dynamic_index_in_dim(child_maps, position, 0, keepdims=False)


def lift_all(coeffs, child_maps):
    grouped = coeffs.reshape(coeffs.shape[0] // 2, 2, coeffs.shape[1], coeffs.shape[2])
    left_part = jnp.einsum(
        "prs,st->prt", grouped[:, 0], child_maps[0], preferred_element_type=jnp.float32
    )
    right_part = jnp.einsum(
        "prs,st->prt", grouped[:, 1], child_maps[1], preferred_element_type=jnp.float32
    )
    return (left_part + right_part).astype(jnp.bfloat16)


def far_term(half_vector, leaf_bases, transfers, couple_list, couple_blocks, first_bit, second_bit):
    coeff_zero = jnp.dot(half_vector, leaf_bases[0], preferred_element_type=jnp.float32).astype(
        jnp.bfloat16
    )
    table_zero = lax.all_gather(coeff_zero[None], "leaf", axis=0, tiled=True)
    table_one = lift_all(table_zero, transfers[0])
    table_two = lift_all(table_one, transfers[1])
    fields = []
    for tree_level, coeff_table in enumerate((table_zero, table_one, table_two)):
        chosen = jnp.take(coeff_table, couple_list[0, tree_level], axis=0)
        fields.append(
            jnp.einsum(
                "krs,kst->rt",
                chosen,
                couple_blocks[0, tree_level],
                preferred_element_type=jnp.float32,
            )
        )
    upper_fields = jnp.stack((fields[1], fields[2]))
    paired = upper_fields + partner(upper_fields, "leaf", 0)
    quad_sum = paired[1] + partner(paired[1], "leaf", 1)
    upper_map = select_map(transfers[1], second_bit).astype(jnp.float32)
    down_one = paired[0] + jnp.dot(quad_sum, upper_map.T, precision=exact_mode)
    lower_map = select_map(transfers[0], first_bit).astype(jnp.float32)
    leaf_field = fields[0] + jnp.dot(down_one, lower_map.T, precision=exact_mode)
    return jnp.einsum(
        "rs,js->rj",
        leaf_field.astype(jnp.bfloat16),
        leaf_bases[0],
        preferred_element_type=jnp.float32,
    )


def shards(
    right_sides,
    near_list,
    near_blocks,
    inverse_list,
    inverse_blocks,
    leaf_bases,
    transfers,
    couple_list,
    couple_blocks,
):
    device_index = lax.axis_index("leaf")
    first_bit = device_index % 2
    second_bit = device_index // 2 % 2
    near_relative = near_list[0] - device_index + REACH
    inverse_relative = inverse_list[0] - device_index + REACH

    def operate(half_vector):
        near_part = apply_slots(neighbourhood(half_vector), near_relative, near_blocks[0])
        far_part = far_term(
            half_vector, leaf_bases, transfers, couple_list, couple_blocks, first_bit, second_bit
        )
        return half_vector.astype(jnp.float32) + near_part + far_part

    def precondition(half_vector):
        return half_vector.astype(jnp.float32) + apply_slots(
            neighbourhood(half_vector), inverse_relative, inverse_blocks[0]
        )

    wide_sides = right_sides.astype(jnp.float32)
    iterate_one = precondition(right_sides)
    residual_one = wide_sides - operate(iterate_one.astype(jnp.bfloat16))
    solution = iterate_one + precondition(residual_one.astype(jnp.bfloat16))
    residual = wide_sides - operate(solution.astype(jnp.bfloat16))
    return (solution, residual)


def solution(mesh):
    return jax.shard_map(
        shards,
        mesh=mesh,
        in_specs=(
            P("parts", "leaf"),
            P(("parts", "leaf"), None),
            P(("parts", "leaf"), None, None, None),
            P(("parts", "leaf"), None),
            P(("parts", "leaf"), None, None, None),
            P(("parts", "leaf"), None, None),
            P(),
            P(("parts", "leaf"), None, None),
            P(("parts", "leaf"), None, None, None, None),
        ),
        out_specs=(P("parts", "leaf"), P("parts", "leaf")),
        check_vma=False,
    )
```

profile of v0, /device:TPU:0, one launch (start us, length us, event | category | flops | bytes accessed | tf_op | source)
XLA Modules:
  0.0 142.7 jit_solution(14897940003670410448)
XLA Ops:
  0.7 5.0 %collective-permute-start = (bf16[64,1024]{1,0:T(8,128)(2,1)}, bf16[64,1024]{1,0:T(8,128)(2,1)S(1)}, u32[]{:S(2)}, u32[]{:S(2)}) collective-permute-start(bf16[64,1024]{1,0:T(8,128)(2,1)} %param.15), channel_id=1, source_target_pairs={{0,2},{1,3},{2,4},{3,5},{4,6},{5,7},{6,8},{7,9},{8,10},{9,11},{10,... | collective-permute-start | bytes 393224 | tf_op jit(solution)/shard_map/ppermute | solution.py:15
  5.7 1.5 %collective-permute-start.1 = (bf16[64,1024]{1,0:T(8,128)(2,1)}, bf16[64,1024]{1,0:T(8,128)(2,1)S(1)}, u32[]{:S(2)}, u32[]{:S(2)}) collective-permute-start(bf16[64,1024]{1,0:T(8,128)(2,1)} %param.15), channel_id=1, source_target_pairs={{0,1},{1,2},{2,3},{3,4},{4,5},{5,6},{6,7},{7,8},{8,9},{9,10},{10,1... | collective-permute-start | bytes 393224 | tf_op jit(solution)/shard_map/ppermute | solution.py:15
  7.2 1.3 collective-permute-start.2
  8.5 1.3 collective-permute-start.3
  9.8 0.7 subtract_add_fusion.1
  10.5 0.6 fusion.200
  11.0 0.7 compare_and_fusion.1
  11.7 0.9 fusion.198
  12.6 0.7 subtract_add_fusion
  13.3 0.7 fusion.199
  23.6 0.9 bitcast_dynamic-update-slice_fusion.17
  24.5 2.1 %fusion.14 = f32[64,1024]{1,0:T(8,128)S(1)} fusion(bf16[1,2,1024,1024]{3,2,1,0:T(8,128)(2,1)} %param.19, bf16[5,64,1024]{2,1,0:T(8,128)(2,1)S(1)} %bitcast_dynamic-update-slice_fusion.15, s32[]{:T(128)S(6)} %select_n.65), kind=kOutput, calls=%fused_computation.20 | convolution fusion | flops 134217728 | bytes 2490372 | tf_op jit(solution)/shard_map/dot_general | solution.py:36
  26.7 2.1 %fusion.201 = (bf16[64,1024]{1,0:T(8,128)(2,1)S(1)}, f32[64,1024]{1,0:T(8,128)S(1)}) fusion(f32[64,1024]{1,0:T(8,128)S(1)} %fusion.14, bf16[1,2,1024,1024]{3,2,1,0:T(8,128)(2,1)} %param.19, bf16[5,64,1024]{2,1,0:T(8,128)(2,1)S(1)} %bitcast_dynamic-update-slice_fusion.15, s32[]{:T(128)S(6)} %select_n.64, bf16[64,1024]{1,0:T(8,128)(2,1)S(1)} %copy-done.2), kind=kOutput, calls=%fused_computation.232 | convolution fusion | flops 134479872 | bytes 3014660 | tf_op jit(solution)/shard_map/dot_general | solution.py:36
  29.0 27.2 %all-gather = bf16[1024,128]{1,0:T(8,128)(2,1)S(1)} all-gather(bf16[64,128]{1,0:T(8,128)(2,1)S(1)} %convolution_convert_fusion.1), channel_id=2, replica_groups=mesh['parts'=2,'leaf'=16] {'leaf'}, dimensions={0}, use_global_device_ids=true | all-gather | bytes 278528 | tf_op jit(solution)/shard_map/all_gather | solution.py:59
  56.8 0.6 gather_fusion.1
  57.4 0.6 gather_fusion.2
  58.4 0.4 collective-permute-start.8
  58.8 1.3 collective-permute-start.4
  60.1 2.1 %collective-permute-start.5 = (bf16[64,1024]{1,0:T(8,128)(2,1)S(1)}, bf16[64,1024]{1,0:T(8,128)(2,1)S(1)}, u32[]{:S(2)}, u32[]{:S(2)}) collective-permute-start(bf16[64,1024]{1,0:T(8,128)(2,1)S(1)} %get-tuple-element.22), channel_id=1, source_target_pairs={{0,1},{1,2},{2,3},{3,4},{4,5},{5,6},{6,7},{7,8},{8,9},{9,10},{10,1... | collective-permute-start | bytes 393224 | tf_op jit(solution)/shard_map/ppermute | solution.py:15
  62.2 1.3 collective-permute-start.6
  63.5 1.3 collective-permute-start.7
  64.8 0.6 gather_fusion
  65.4 3.7 %collective-permute-start.9 = (f32[64,128]{1,0:T(8,128)S(1)}, f32[64,128]{1,0:T(8,128)S(1)}, u32[]{:S(2)}, u32[]{:S(2)}) collective-permute-start(f32[64,128]{1,0:T(8,128)S(1)} %slice_bitcast_fusion.18), channel_id=1, source_target_pairs={{0,2},{1,3},{2,0},{3,1},{4,6},{5,7},{6,4},{7,5},{8,10},{9,11},{10,... | collective-permute-start | bytes 98312 | tf_op jit(solution)/shard_map/ppermute | solution.py:21
  69.3 3.6 %collective-permute-done.9 = f32[64,128]{1,0:T(8,128)S(1)} collective-permute-done((f32[64,128]{1,0:T(8,128)S(1)}, f32[64,128]{1,0:T(8,128)S(1)}, u32[]{:S(2)}, u32[]{:S(2)}) %collective-permute-start.9) | collective-permute-done | bytes 32800 | tf_op jit(solution)/shard_map/ppermute | solution.py:21
  73.7 2.1 %fusion.2 = f32[64,1024]{1,0:T(8,128)S(1)} fusion(bf16[1,3,1024,1024]{3,2,1,0:T(8,128)(2,1)} %param.17, bf16[5,64,1024]{2,1,0:T(8,128)(2,1)S(1)} %bitcast_dynamic-update-slice_fusion.10, s32[]{:T(128)S(6)} %select_n.68), kind=kOutput, calls=%fused_computation.8 | convolution fusion | flops 134217728 | bytes 2490372 | tf_op jit(solution)/shard_map/dot_general | solution.py:36
  75.8 2.2 %fusion.6 = f32[64,1024]{1,0:T(8,128)S(1)} fusion(bf16[1,3,1024,1024]{3,2,1,0:T(8,128)(2,1)} %param.17, bf16[5,64,1024]{2,1,0:T(8,128)(2,1)S(1)} %bitcast_dynamic-update-slice_fusion.10, s32[]{:T(128)S(6)} %select_n.67), kind=kOutput, calls=%fused_computation.12 | convolution fusion | flops 134217728 | bytes 2490372 | tf_op jit(solution)/shard_map/dot_general | solution.py:36
  78.0 2.1 %fusion.77 = bf16[64,1024]{1,0:T(8,128)(2,1)S(1)} fusion(f32[64,1024]{1,0:T(8,128)S(1)} %fusion.87, f32[64,1024]{1,0:T(8,128)S(1)} %fusion.2, f32[64,1024]{1,0:T(8,128)S(1)} %fusion.6, bf16[1,3,1024,1024]{3,2,1,0:T(8,128)(2,1)} %param.17, bf16[64,1024]{1,0:T(8,128)(2,1)S(1)} %copy-done.2, bf16[64,1024]{1,0:T(8,128)(2,1)S(1)} %get-tuple-element.22, ...), kind=kOutput, calls=%fused_computation.55 | convolution fusion | flops 134742016 | bytes 3407876 | tf_op jit(solution)/shard_map/dot_general | solution.py:36
  80.2 3.4 %collective-permute-start.10 = (bf16[64,1024]{1,0:T(8,128)(2,1)S(1)}, bf16[64,1024]{1,0:T(8,128)(2,1)S(1)}, u32[]{:S(2)}, u32[]{:S(2)}) collective-permute-start(bf16[64,1024]{1,0:T(8,128)(2,1)S(1)} %fusion.77), channel_id=1, source_target_pairs={{0,2},{1,3},{2,4},{3,5},{4,6},{5,7},{6,8},{7,9},{8,10},{9,11},{10,... | collective-permute-start | bytes 393224 | tf_op jit(solution)/shard_map/ppermute | solution.py:15
  83.6 1.3 collective-permute-start.11
  84.9 1.3 collective-permute-start.12
  86.2 1.3 collective-permute-start.13
  87.6 2.3 %collective-permute-done.12 = bf16[64,1024]{1,0:T(8,128)(2,1)S(1)} collective-permute-done((bf16[64,1024]{1,0:T(8,128)(2,1)S(1)}, bf16[64,1024]{1,0:T(8,128)(2,1)S(1)}, u32[]{:S(2)}, u32[]{:S(2)}) %collective-permute-start.12) | collective-permute-done | bytes 131104 | tf_op jit(solution)/shard_map/ppermute | solution.py:15
  89.9 6.5 %collective-permute-done.13 = bf16[64,1024]{1,0:T(8,128)(2,1)S(1)} collective-permute-done((bf16[64,1024]{1,0:T(8,128)(2,1)S(1)}, bf16[64,1024]{1,0:T(8,128)(2,1)S(1)}, u32[]{:S(2)}, u32[]{:S(2)}) %collective-permute-start.13) | collective-permute-done | bytes 131104 | tf_op jit(solution)/shard_map/ppermute | solution.py:15
  96.4 0.5 fusion.12
  96.9 1.2 fusion.202
  98.3 19.8 %all-gather.1 = bf16[1024,128]{1,0:T(8,128)(2,1)S(1)} all-gather(bf16[64,128]{1,0:T(8,128)(2,1)S(1)} %convolution_convert_fusion), channel_id=3, replica_groups=mesh['parts'=2,'leaf'=16] {'leaf'}, dimensions={0}, use_global_device_ids=true | all-gather | bytes 278528 | tf_op jit(solution)/shard_map/all_gather | solution.py:59
  118.5 0.6 gather_fusion.4
  119.3 0.6 gather_fusion.5
  120.8 1.9 %collective-permute-start.14 = (bf16[64,1024]{1,0:T(8,128)(2,1)S(1)}, bf16[64,1024]{1,0:T(8,128)(2,1)S(1)}, u32[]{:S(2)}, u32[]{:S(2)}) collective-permute-start(bf16[64,1024]{1,0:T(8,128)(2,1)S(1)} %get-tuple-element.24), channel_id=1, source_target_pairs={{0,2},{1,3},{2,4},{3,5},{4,6},{5,7},{6,8},{7,9},{8,10},{9,11},{10,... | collective-permute-start | bytes 393224 | tf_op jit(solution)/shard_map/ppermute | solution.py:15
  122.7 1.8 %collective-permute-start.15 = (bf16[64,1024]{1,0:T(8,128)(2,1)S(1)}, bf16[64,1024]{1,0:T(8,128)(2,1)S(1)}, u32[]{:S(2)}, u32[]{:S(2)}) collective-permute-start(bf16[64,1024]{1,0:T(8,128)(2,1)S(1)} %get-tuple-element.24), channel_id=1, source_target_pairs={{0,1},{1,2},{2,3},{3,4},{4,5},{5,6},{6,7},{7,8},{8,9},{9,10},{10,1... | collective-permute-start | bytes 393224 | tf_op jit(solution)/shard_map/ppermute | solution.py:15
  124.5 1.3 collective-permute-start.16
  125.8 1.3 collective-permute-start.17
  127.1 0.6 gather_fusion.3
  127.7 3.4 %collective-permute-start.19 = (f32[64,128]{1,0:T(8,128)S(1)}, f32[64,128]{1,0:T(8,128)S(1)}, u32[]{:S(2)}, u32[]{:S(2)}) collective-permute-start(f32[64,128]{1,0:T(8,128)S(1)} %slice_bitcast_fusion.16), channel_id=1, source_target_pairs={{0,2},{1,3},{2,0},{3,1},{4,6},{5,7},{6,4},{7,5},{8,10},{9,11},{10,... | collective-permute-start | bytes 98312 | tf_op jit(solution)/shard_map/ppermute | solution.py:21
  131.3 3.6 %collective-permute-done.19 = f32[64,128]{1,0:T(8,128)S(1)} collective-permute-done((f32[64,128]{1,0:T(8,128)S(1)}, f32[64,128]{1,0:T(8,128)S(1)}, u32[]{:S(2)}, u32[]{:S(2)}) %collective-permute-start.19) | collective-permute-done | bytes 32800 | tf_op jit(solution)/shard_map/ppermute | solution.py:21
  135.7 2.1 %fusion = f32[64,1024]{1,0:T(8,128)S(1)} fusion(bf16[1,3,1024,1024]{3,2,1,0:T(8,128)(2,1)} %param.17, bf16[5,64,1024]{2,1,0:T(8,128)(2,1)S(1)} %bitcast_dynamic-update-slice_fusion, s32[]{:T(128)S(6)} %select_n.68), kind=kOutput, calls=%fused_computation.6 | convolution fusion | flops 134217728 | bytes 2490372 | tf_op jit(solution)/shard_map/dot_general | solution.py:36
  137.7 2.1 %fusion.4 = f32[64,1024]{1,0:T(8,128)S(1)} fusion(bf16[1,3,1024,1024]{3,2,1,0:T(8,128)(2,1)} %param.17, bf16[5,64,1024]{2,1,0:T(8,128)(2,1)S(1)} %bitcast_dynamic-update-slice_fusion, s32[]{:T(128)S(6)} %select_n.67), kind=kOutput, calls=%fused_computation.10 | convolution fusion | flops 134217728 | bytes 2490372 | tf_op jit(solution)/shard_map/dot_general | solution.py:36
  139.8 2.8 %fusion.72 = f32[64,1024]{1,0:T(8,128)} fusion(f32[64,1024]{1,0:T(8,128)S(1)} %fusion.84, f32[64,1024]{1,0:T(8,128)S(1)} %fusion, f32[64,1024]{1,0:T(8,128)S(1)} %fusion.4, bf16[1,3,1024,1024]{3,2,1,0:T(8,128)(2,1)} %param.17, bf16[64,1024]{1,0:T(8,128)(2,1)S(1)} %copy-done.2, bf16[64,1024]{1,0:T(8,128)(2,1)S(1)} %get-tuple-element.24, ...), kind=kOutput, calls=%fused_computation.52 | convolution fusion | flops 134676480 | bytes 3538948 | tf_op jit(solution)/shard_map/dot_general | solution.py:36
  (77 shorter events, 4.8 us)
Async XLA Ops:
  0.6 28.1 %copy-start = (bf16[1,1024,128]{2,1,0:T(8,128)(2,1)S(1)}, bf16[1,1024,128]{2,1,0:T(8,128)(2,1)}, u32[]{:S(2)}) copy-start(bf16[1,1024,128]{2,1,0:T(8,128)(2,1)} %param.20) | copy-start | bytes 786436
  0.6 26.0 %copy-start.2 = (bf16[64,1024]{1,0:T(8,128)(2,1)S(1)}, bf16[64,1024]{1,0:T(8,128)(2,1)}, u32[]{:S(2)}) copy-start(bf16[64,1024]{1,0:T(8,128)(2,1)} %param.15) | copy-start | bytes 393220
  0.7 55.5 %copy-start.3 = (bf16[2,2,128,128]{3,2,1,0:T(8,128)(2,1)S(1)}, bf16[2,2,128,128]{3,2,1,0:T(8,128)(2,1)}, u32[]{:S(2)}) copy-start(bf16[2,2,128,128]{3,2,1,0:T(8,128)(2,1)} %param.21) | copy-start | bytes 393220
  0.7 22.8 %collective-permute-start = (bf16[64,1024]{1,0:T(8,128)(2,1)}, bf16[64,1024]{1,0:T(8,128)(2,1)S(1)}, u32[]{:S(2)}, u32[]{:S(2)}) collective-permute-start(bf16[64,1024]{1,0:T(8,128)(2,1)} %param.15), channel_id=1, source_target_pairs={{0,2},{1,3},{2,4},{3,5},{4,6},{5,7},{6,8},{7,9},{8,10},{9,11},{10,... | collective-permute-start | bytes 393224 | tf_op jit(solution)/shard_map/ppermute | solution.py:15
  5.7 17.8 %collective-permute-start.1 = (bf16[64,1024]{1,0:T(8,128)(2,1)}, bf16[64,1024]{1,0:T(8,128)(2,1)S(1)}, u32[]{:S(2)}, u32[]{:S(2)}) collective-permute-start(bf16[64,1024]{1,0:T(8,128)(2,1)} %param.15), channel_id=1, source_target_pairs={{0,1},{1,2},{2,3},{3,4},{4,5},{5,6},{6,7},{7,8},{8,9},{9,10},{10,1... | collective-permute-start | bytes 393224 | tf_op jit(solution)/shard_map/ppermute | solution.py:15
  7.2 17.3 %collective-permute-start.2 = (bf16[64,1024]{1,0:T(8,128)(2,1)}, bf16[64,1024]{1,0:T(8,128)(2,1)S(1)}, u32[]{:S(2)}, u32[]{:S(2)}) collective-permute-start(bf16[64,1024]{1,0:T(8,128)(2,1)} %param.15), channel_id=1, source_target_pairs={{1,0},{2,1},{3,2},{4,3},{5,4},{6,5},{7,6},{8,7},{9,8},{10,9},{11,1... | collective-permute-start | bytes 393224 | tf_op jit(solution)/shard_map/ppermute | solution.py:15
  8.5 16.0 %collective-permute-start.3 = (bf16[64,1024]{1,0:T(8,128)(2,1)}, bf16[64,1024]{1,0:T(8,128)(2,1)S(1)}, u32[]{:S(2)}, u32[]{:S(2)}) collective-permute-start(bf16[64,1024]{1,0:T(8,128)(2,1)} %param.15), channel_id=1, source_target_pairs={{2,0},{3,1},{4,2},{5,3},{6,4},{7,5},{8,6},{9,7},{10,8},{11,9},{12,... | collective-permute-start | bytes 393224 | tf_op jit(solution)/shard_map/ppermute | solution.py:15
  24.5 33.4 %copy-start.4 = (bf16[1,3,4,128,128]{4,3,2,1,0:T(8,128)(2,1)S(1)}, bf16[1,3,4,128,128]{4,3,2,1,0:T(8,128)(2,1)}, u32[]{:S(2)}) copy-start(bf16[1,3,4,128,128]{4,3,2,1,0:T(8,128)(2,1)} %param.23) | copy-start | bytes 1179652
  58.4 7.0 %collective-permute-start.8 = (f32[2,64,128]{2,1,0:T(8,128)S(1)}, f32[2,64,128]{2,1,0:T(8,128)S(1)}, u32[]{:S(2)}, u32[]{:S(2)}) collective-permute-start(f32[2,64,128]{2,1,0:T(8,128)S(1)} %pad_maximum_fusion), channel_id=1, source_target_pairs={{0,1},{1,0},{2,3},{3,2},{4,5},{5,4},{6,7},{7,6},{8,9},{9,8},{10,11... | collective-permute-start | bytes 196616 | tf_op jit(solution)/shard_map/ppermute | solution.py:21
  58.8 14.8 %collective-permute-start.4 = (bf16[64,1024]{1,0:T(8,128)(2,1)S(1)}, bf16[64,1024]{1,0:T(8,128)(2,1)S(1)}, u32[]{:S(2)}, u32[]{:S(2)}) collective-permute-start(bf16[64,1024]{1,0:T(8,128)(2,1)S(1)} %get-tuple-element.22), channel_id=1, source_target_pairs={{0,2},{1,3},{2,4},{3,5},{4,6},{5,7},{6,8},{7,9},{8,10},{9,11},{10,... | collective-permute-start | bytes 393224 | tf_op jit(solution)/shard_map/ppermute | solution.py:15
  60.1 13.5 %collective-permute-start.5 = (bf16[64,1024]{1,0:T(8,128)(2,1)S(1)}, bf16[64,1024]{1,0:T(8,128)(2,1)S(1)}, u32[]{:S(2)}, u32[]{:S(2)}) collective-permute-start(bf16[64,1024]{1,0:T(8,128)(2,1)S(1)} %get-tuple-element.22), channel_id=1, source_target_pairs={{0,1},{1,2},{2,3},{3,4},{4,5},{5,6},{6,7},{7,8},{8,9},{9,10},{10,1... | collective-permute-start | bytes 393224 | tf_op jit(solution)/shard_map/ppermute | solution.py:15
  62.2 11.5 %collective-permute-start.6 = (bf16[64,1024]{1,0:T(8,128)(2,1)S(1)}, bf16[64,1024]{1,0:T(8,128)(2,1)S(1)}, u32[]{:S(2)}, u32[]{:S(2)}) collective-permute-start(bf16[64,1024]{1,0:T(8,128)(2,1)S(1)} %get-tuple-element.22), channel_id=1, source_target_pairs={{1,0},{2,1},{3,2},{4,3},{5,4},{6,5},{7,6},{8,7},{9,8},{10,9},{11,1... | collective-permute-start | bytes 393224 | tf_op jit(solution)/shard_map/ppermute | solution.py:15
  63.5 10.2 %collective-permute-start.7 = (bf16[64,1024]{1,0:T(8,128)(2,1)S(1)}, bf16[64,1024]{1,0:T(8,128)(2,1)S(1)}, u32[]{:S(2)}, u32[]{:S(2)}) collective-permute-start(bf16[64,1024]{1,0:T(8,128)(2,1)S(1)} %get-tuple-element.22), channel_id=1, source_target_pairs={{2,0},{3,1},{4,2},{5,3},{6,4},{7,5},{8,6},{9,7},{10,8},{11,9},{12,... | collective-permute-start | bytes 393224 | tf_op jit(solution)/shard_map/ppermute | solution.py:15
  65.4 7.6 %collective-permute-start.9 = (f32[64,128]{1,0:T(8,128)S(1)}, f32[64,128]{1,0:T(8,128)S(1)}, u32[]{:S(2)}, u32[]{:S(2)}) collective-permute-start(f32[64,128]{1,0:T(8,128)S(1)} %slice_bitcast_fusion.18), channel_id=1, source_target_pairs={{0,2},{1,3},{2,0},{3,1},{4,6},{5,7},{6,4},{7,5},{8,10},{9,11},{10,... | collective-permute-start | bytes 98312 | tf_op jit(solution)/shard_map/ppermute | solution.py:21
  75.8 20.6 %copy-start.1 = (bf16[1,2,1024,1024]{3,2,1,0:T(8,128)(2,1)S(1)}, bf16[1,2,1024,1024]{3,2,1,0:T(8,128)(2,1)}, u32[]{:S(2)}) copy-start(bf16[1,2,1024,1024]{3,2,1,0:T(8,128)(2,1)} %param.19) | copy-start | bytes 12582916
  80.2 7.3 %collective-permute-start.10 = (bf16[64,1024]{1,0:T(8,128)(2,1)S(1)}, bf16[64,1024]{1,0:T(8,128)(2,1)S(1)}, u32[]{:S(2)}, u32[]{:S(2)}) collective-permute-start(bf16[64,1024]{1,0:T(8,128)(2,1)S(1)} %fusion.77), channel_id=1, source_target_pairs={{0,2},{1,3},{2,4},{3,5},{4,6},{5,7},{6,8},{7,9},{8,10},{9,11},{10,... | collective-permute-start | bytes 393224 | tf_op jit(solution)/shard_map/ppermute | solution.py:15
  83.6 3.9 %collective-permute-start.11 = (bf16[64,1024]{1,0:T(8,128)(2,1)S(1)}, bf16[64,1024]{1,0:T(8,128)(2,1)S(1)}, u32[]{:S(2)}, u32[]{:S(2)}) collective-permute-start(bf16[64,1024]{1,0:T(8,128)(2,1)S(1)} %fusion.77), channel_id=1, source_target_pairs={{0,1},{1,2},{2,3},{3,4},{4,5},{5,6},{6,7},{7,8},{8,9},{9,10},{10,1... | collective-permute-start | bytes 393224 | tf_op jit(solution)/shard_map/ppermute | solution.py:15
  84.9 5.0 %collective-permute-start.12 = (bf16[64,1024]{1,0:T(8,128)(2,1)S(1)}, bf16[64,1024]{1,0:T(8,128)(2,1)S(1)}, u32[]{:S(2)}, u32[]{:S(2)}) collective-permute-start(bf16[64,1024]{1,0:T(8,128)(2,1)S(1)} %fusion.77), channel_id=1, source_target_pairs={{1,0},{2,1},{3,2},{4,3},{5,4},{6,5},{7,6},{8,7},{9,8},{10,9},{11,1... | collective-permute-start | bytes 393224 | tf_op jit(solution)/shard_map/ppermute | solution.py:15
  86.2 10.2 %collective-permute-start.13 = (bf16[64,1024]{1,0:T(8,128)(2,1)S(1)}, bf16[64,1024]{1,0:T(8,128)(2,1)S(1)}, u32[]{:S(2)}, u32[]{:S(2)}) collective-permute-start(bf16[64,1024]{1,0:T(8,128)(2,1)S(1)} %fusion.77), channel_id=1, source_target_pairs={{2,0},{3,1},{4,2},{5,3},{6,4},{7,5},{8,6},{9,7},{10,8},{11,9},{12,... | collective-permute-start | bytes 393224 | tf_op jit(solution)/shard_map/ppermute | solution.py:15
  120.3 7.3 %collective-permute-start.18 = (f32[2,64,128]{2,1,0:T(8,128)S(1)}, f32[2,64,128]{2,1,0:T(8,128)S(1)}, u32[]{:S(2)}, u32[]{:S(2)}) collective-permute-start(f32[2,64,128]{2,1,0:T(8,128)S(1)} %pad_maximum_fusion.1), channel_id=1, source_target_pairs={{0,1},{1,0},{2,3},{3,2},{4,5},{5,4},{6,7},{7,6},{8,9},{9,8},{10,11... | collective-permute-start | bytes 196616 | tf_op jit(solution)/shard_map/ppermute | solution.py:21
  120.8 14.8 %collective-permute-start.14 = (bf16[64,1024]{1,0:T(8,128)(2,1)S(1)}, bf16[64,1024]{1,0:T(8,128)(2,1)S(1)}, u32[]{:S(2)}, u32[]{:S(2)}) collective-permute-start(bf16[64,1024]{1,0:T(8,128)(2,1)S(1)} %get-tuple-element.24), channel_id=1, source_target_pairs={{0,2},{1,3},{2,4},{3,5},{4,6},{5,7},{6,8},{7,9},{8,10},{9,11},{10,... | collective-permute-start | bytes 393224 | tf_op jit(solution)/shard_map/ppermute | solution.py:15
  122.7 12.9 %collective-permute-start.15 = (bf16[64,1024]{1,0:T(8,128)(2,1)S(1)}, bf16[64,1024]{1,0:T(8,128)(2,1)S(1)}, u32[]{:S(2)}, u32[]{:S(2)}) collective-permute-start(bf16[64,1024]{1,0:T(8,128)(2,1)S(1)} %get-tuple-element.24), channel_id=1, source_target_pairs={{0,1},{1,2},{2,3},{3,4},{4,5},{5,6},{6,7},{7,8},{8,9},{9,10},{10,1... | collective-permute-start | bytes 393224 | tf_op jit(solution)/shard_map/ppermute | solution.py:15
  124.5 11.1 %collective-permute-start.16 = (bf16[64,1024]{1,0:T(8,128)(2,1)S(1)}, bf16[64,1024]{1,0:T(8,128)(2,1)S(1)}, u32[]{:S(2)}, u32[]{:S(2)}) collective-permute-start(bf16[64,1024]{1,0:T(8,128)(2,1)S(1)} %get-tuple-element.24), channel_id=1, source_target_pairs={{1,0},{2,1},{3,2},{4,3},{5,4},{6,5},{7,6},{8,7},{9,8},{10,9},{11,1... | collective-permute-start | bytes 393224 | tf_op jit(solution)/shard_map/ppermute | solution.py:15
  125.8 9.9 %collective-permute-start.17 = (bf16[64,1024]{1,0:T(8,128)(2,1)S(1)}, bf16[64,1024]{1,0:T(8,128)(2,1)S(1)}, u32[]{:S(2)}, u32[]{:S(2)}) collective-permute-start(bf16[64,1024]{1,0:T(8,128)(2,1)S(1)} %get-tuple-element.24), channel_id=1, source_target_pairs={{2,0},{3,1},{4,2},{5,3},{6,4},{7,5},{8,6},{9,7},{10,8},{11,9},{12,... | collective-permute-start | bytes 393224 | tf_op jit(solution)/shard_map/ppermute | solution.py:15
  127.7 7.2 %collective-permute-start.19 = (f32[64,128]{1,0:T(8,128)S(1)}, f32[64,128]{1,0:T(8,128)S(1)}, u32[]{:S(2)}, u32[]{:S(2)}) collective-permute-start(f32[64,128]{1,0:T(8,128)S(1)} %slice_bitcast_fusion.16), channel_id=1, source_target_pairs={{0,2},{1,3},{2,0},{3,1},{4,6},{5,7},{6,4},{7,5},{8,10},{9,11},{10,... | collective-permute-start | bytes 98312 | tf_op jit(solution)/shard_map/ppermute | solution.py:21
where the time goes:
time: 144 us; the launch traced here: 143 us
  blocking collectives  47 us (33%)
  starting transfers between devices  36.5 us (25%)
  matrix products  23.3 us (16%)
  waiting for transfers between devices  16.1 us (11%)
  between operations  10.9 us (8%)
  local copies, waits for them, and re-layouts  6.68 us (5%)
  other arithmetic  2.07 us (1%)
    all_gather x2, blocking collectives, far_term(): table_zero = lax.all_gather(coeff_zero[None], 'leaf', axis=0, tiled=True)  47 us
    ppermute x16, starting transfers between devices, from_behind(): lax.ppermute(value, axis, [(source, source + steps) for source in range(f...  28.6 us
    dot_general x10, matrix products, apply_slots(): jnp.dot(chosen, blocks[slot_index], preferred_element_type=jnp.float32)  19.3 us
    ppermute x16, waiting for transfers between devices, from_behind(): lax.ppermute(value, axis, [(source, source + steps) for source in range(f...  8.85 us
    ppermute x4, starting transfers between devices, partner(): return lax.ppermute(value, axis, pairs)  7.94 us
    ppermute x4, waiting for transfers between devices, partner(): return lax.ppermute(value, axis, pairs)  7.25 us
    gather x6, local copies, waits for them, and re-layouts, far_term(): chosen = jnp.take(coeff_table, couple_list[0, tree_level], axis=0)  3.38 us
  transfers between devices with their start and end apart: 20, of which 4 were waited for; matrix products, arithmetic and copies ran while one was open for 6% of the time, Pallas kernels for 0%

commit v1 on v0

v1 whole, which is shorter than its diff:
```python
import functools

import jax
import jax.numpy as jnp
from jax import lax
from jax.experimental import pallas as pl
from jax.experimental.pallas import tpu as pltpu
from jax.sharding import PartitionSpec as P

REACH = 2
F32 = jnp.float32
BF16 = jnp.bfloat16
VM = pl.BlockSpec(memory_space=pltpu.VMEM)
SM = pl.BlockSpec(memory_space=pltpu.SMEM)


def swap(value, pairs):
    return lax.ppermute(value, "leaf", pairs)


def xor_pairs(count, mask):
    return [(source, source ^ mask) for source in range(count)]


def odd_edges(count):
    inner = [(source, source + 2 if source & 2 else source - 2) for source in range(2, count - 2)]
    ends = [(0, 1), (1, 0), (count - 2, count - 1), (count - 1, count - 2)]
    return inner + ends


def split_pairs(count, mask):
    return [(source, source ^ mask ^ (2 * (source & 1))) for source in range(count)]


def window_slot(relative, place):
    core, side = place % 2, place // 2 % 2
    left, right = jnp.where(side == 0, 3, 2), jnp.where(side == 0, 2, 3)
    near = jnp.where((relative == 1) == (core == 0), 1, 4)
    far = jnp.where(relative < 0, left, right)
    return jnp.where(relative == 0, 0, jnp.where(abs(relative) == 1, near, far))


def exchange(value, count):
    place = lax.axis_index("leaf")
    core, side = place % 2, place // 2 % 2
    odd = swap(value, odd_edges(count))
    even = swap(value, xor_pairs(count, 2))
    partner = swap(value, xor_pairs(count, 1))
    forward = swap(jnp.where(core == side, even, odd), xor_pairs(count, 1))
    return value, partner, even, odd, forward


def block_sum(place, list_ref, pieces, stack, blocks, slots):
    for index, piece in enumerate(pieces):
        stack[index] = piece[:, : stack.shape[2]]
    total = None
    for slot in range(slots):
        spot = window_slot(list_ref[0, slot] - place, place)
        part = jnp.dot(stack[spot], blocks[slot], preferred_element_type=F32)
        total = part if total is None else total + part
    return total


def smooth_kernel(has_base, place_ref, list_ref, *refs):
    pieces, refs = refs[:5], refs[5:]
    if has_base:
        base, refs = refs[0], refs[1:]
    blocks, bases, wide, half, coeff, stack = refs
    place = place_ref[0]
    total = block_sum(place, list_ref, pieces, stack, blocks, blocks.shape[0])
    total = total + pieces[0][...].astype(F32)
    if has_base:
        total = total + base[...]
    wide[...] = total
    rounded = total.astype(BF16)
    size = rounded.shape[1]
    half[:, :size] = rounded
    coeffs = jnp.dot(rounded, bases[...], preferred_element_type=F32).astype(BF16)
    half[:, size:] = coeffs
    coeff[...] = coeffs


def near_kernel(place_ref, list_ref, *refs):
    pieces, (sides, blocks, out, stack) = refs[:5], refs[5:]
    total = block_sum(place_ref[0], list_ref, pieces, stack, blocks, blocks.shape[0])
    size = stack.shape[2]
    out[...] = sides[...].astype(F32) - pieces[0][:, :size].astype(F32) - total


def far_kernel(offsets, place_ref, *refs):
    tables, (kernel_map, bases, partial, out) = refs[: len(offsets)], refs[len(offsets) :]
    place = place_ref[0]
    core = place % 2
    field = None
    for table, offset in zip(tables, offsets):
        for row in range(table.shape[0]):
            leaf = offset(place, core, row)
            part = jnp.dot(table[row], kernel_map[leaf], preferred_element_type=F32)
            field = part if field is None else field + part
    far = lax.dot_general(
        field.astype(BF16), bases[...], (((1,), (1,)), ((), ())), preferred_element_type=F32
    )
    out[...] = (partial[...] - far).astype(out.dtype)


def far_loop_kernel(place_ref, table, kernel_map, bases, partial, out):
    def step(leaf, field):
        return field + jnp.dot(table[leaf], kernel_map[leaf], preferred_element_type=F32)

    field = lax.fori_loop(0, table.shape[0], step, jnp.zeros(table.shape[1:], F32))
    far = lax.dot_general(
        field.astype(BF16), bases[...], (((1,), (1,)), ((), ())), preferred_element_type=F32
    )
    out[...] = (partial[...] - far).astype(out.dtype)


def scatter_kernel(list_ref, blocks, pair_out, quad_out, pair_sum, quad_sum):
    for level, total, out in ((1, pair_sum, pair_out), (2, quad_sum, quad_out)):
        total[...] = jnp.zeros_like(total)
        for slot in range(blocks.shape[1]):
            cluster = list_ref[0, level, slot]
            total[cluster] += blocks[level, slot].astype(F32)
        out[...] = total[...].astype(out.dtype)


def fold_kernel(place_ref, list_ref, blocks, maps, pair_a, pair_b, quads, out, total):
    place = place_ref[0]
    first, second = place % 2, place // 2 % 2
    total[...] = jnp.zeros_like(total)
    for slot in range(blocks.shape[1]):
        total[list_ref[0, 0, slot]] += blocks[0, slot].astype(F32)

    def turned(left, child_map):
        return lax.dot_general(
            left.astype(BF16), child_map, (((1,), (1,)), ((), ())), preferred_element_type=F32
        )

    def step(quad, carry):
        coarse = sum(ref[quad].astype(F32) for ref in quads)
        coarse = turned(coarse, maps[1, second]).astype(BF16)
        for half in range(2):
            pair = 2 * quad + half
            middle = jnp.dot(maps[1, half], coarse, preferred_element_type=F32)
            middle = middle + pair_a[pair].astype(F32) + pair_b[pair].astype(F32)
            middle = turned(middle, maps[0, first]).astype(BF16)
            for child in range(2):
                leaf = 2 * pair + child
                fine = jnp.dot(maps[0, child], middle, preferred_element_type=F32)
                out[leaf] = (fine + total[leaf]).astype(BF16)
        return carry

    lax.fori_loop(0, out.shape[0] // 4, step, 0)


def shards(
    count,
    right_sides,
    near_list,
    near_blocks,
    inverse_list,
    inverse_blocks,
    leaf_bases,
    transfers,
    couple_list,
    couple_blocks,
):
    rows, size = right_sides.shape
    rank = leaf_bases.shape[2]
    place = lax.axis_index("leaf")
    place_ref = place.astype(jnp.int32).reshape(1)
    near, inverse, bases, couples = near_blocks[0], inverse_blocks[0], leaf_bases[0], couple_blocks[0]
    shape = jax.ShapeDtypeStruct
    one = xor_pairs(count, 1)

    def call(kernel, out_shape, scratch, ints, *operands):
        return pl.pallas_call(
            kernel,
            out_shape=out_shape,
            in_specs=[SM] * ints + [VM] * (len(operands) - ints),
            out_specs=jax.tree.map(lambda _: VM, out_shape),
            scratch_shapes=scratch,
            compiler_params=pltpu.CompilerParams(vmem_limit_bytes=24 << 20),
        )(*operands)

    window = [pltpu.VMEM((5, rows, size), BF16)]

    def smooth(pieces, base):
        extra = () if base is None else (base,)
        return call(
            functools.partial(smooth_kernel, base is not None),
            (shape((rows, size), F32), shape((rows, size + rank), BF16), shape((rows, rank), BF16)),
            window,
            2,
            place_ref,
            inverse_list,
            *pieces,
            *extra,
            inverse,
            bases,
        )

    def gather(coeff, half, even):
        if count != 16:
            return [lax.all_gather(coeff, "leaf", axis=0)], None
        other = swap(coeff, one)
        both = jnp.stack([coeff, other])
        masks = (12, 8, 4)
        got = [swap(both, split_pairs(count, mask)) for mask in masks]
        mine = jnp.concatenate([even[None, :, size:]] + got)
        theirs = swap(mine, one)

        def of_pair(place, core, row):
            return place ^ row

        def of_mine(place, core, row):
            if row == 0:
                return place ^ 2
            return place ^ masks[(row - 1) // 2] ^ (2 * core) ^ ((row - 1) % 2)

        def of_theirs(place, core, row):
            return of_mine(place ^ 1, 1 - core, row)

        return [both, mine, theirs], [of_pair, of_mine, of_theirs]

    def operate(half, coeff, kernel_map, dtype):
        pieces = exchange(half, count)
        tables, offsets = gather(coeff, half, pieces[2])
        partial = call(
            near_kernel,
            shape((rows, size), F32),
            window,
            2,
            place_ref,
            near_list,
            *pieces,
            right_sides,
            near,
        )
        kernel = far_loop_kernel if offsets is None else functools.partial(far_kernel, offsets)
        return call(
            kernel, shape((rows, size), dtype), [], 1, place_ref, *tables, kernel_map, bases, partial
        )

    pieces = exchange(right_sides, count)
    pair_own, quad_own = call(
        scatter_kernel,
        (shape((count // 2, rank, rank), BF16), shape((count // 4, rank, rank), BF16)),
        [pltpu.VMEM((count // 2, rank, rank), F32), pltpu.VMEM((count // 4, rank, rank), F32)],
        1,
        couple_list,
        couples,
    )
    quad_side = swap(quad_own, xor_pairs(count, 2))
    pair_other, quad_other, quad_cross = swap(pair_own, one), swap(quad_own, one), swap(quad_side, one)

    def fold(place_ref, list_ref, blocks, maps, pair_a, pair_b, qa, qb, qc, qd, out, total):
        fold_kernel(place_ref, list_ref, blocks, maps, pair_a, pair_b, (qa, qb, qc, qd), out, total)

    kernel_map = call(
        fold,
        shape((count, rank, rank), BF16),
        [pltpu.VMEM((count, rank, rank), F32)],
        2,
        place_ref,
        couple_list,
        couples,
        transfers,
        pair_own,
        pair_other,
        quad_own,
        quad_side,
        quad_other,
        quad_cross,
    )
    first, first_half, first_coeff = smooth(pieces, None)
    left = operate(first_half, first_coeff, kernel_map, BF16)
    second, second_half, second_coeff = smooth(exchange(left, count), first)
    residual = operate(second_half, second_coeff, kernel_map, F32)
    return second, residual


def solution(mesh):
    return jax.shard_map(
        functools.partial(shards, mesh.shape["leaf"]),
        mesh=mesh,
        in_specs=(
            P("parts", "leaf"),
            P(("parts", "leaf"), None),
            P(("parts", "leaf"), None, None, None),
            P(("parts", "leaf"), None),
            P(("parts", "leaf"), None, None, None),
            P(("parts", "leaf"), None, None),
            P(),
            P(("parts", "leaf"), None, None),
            P(("parts", "leaf"), None, None, None, None),
        ),
        out_specs=(P("parts", "leaf"), P("parts", "leaf")),
        check_vma=False,
    )
```

time: 144 us -> 75.8 us (0.53)
  blocking collectives: 47 us -> 0 us
  matrix products: 23.3 us -> 0 us
  Pallas kernels: 0 us -> 13.5 us
  between operations: 10.9 us -> 0.89 us
  starting transfers between devices: 36.5 us -> 33.6 us
  local copies, waits for them, and re-layouts: 6.68 us -> 9.2 us
  waiting for transfers between devices: 16.1 us -> 18.1 us
  other arithmetic: 2.07 us -> 0.11 us
    all_gather x2 -> x0, blocking collectives: 47 us -> none  [far_term(): table_zero = lax.all_gather(coeff_zero[None], 'leaf', axis=0, tiled=True)]
    dot_general x32 -> x0, matrix products: 23.3 us -> none  [the longest x10 19.3 us: apply_slots(): jnp.dot(chosen, blocks[slot_index], preferred_element_type=jnp.float32)]
    pallas_call x0 -> x8, Pallas kernels: none -> 13.5 us  [call(): pl.pallas_call(kernel, out_shape=out_shape, in_specs=[SM] * ints + [VM] *...]
    unnamed x26 -> x29, local copies, waits for them, and re-layouts: 1.11 us -> 9.2 us
    gather x6 -> x0, local copies, waits for them, and re-layouts: 3.38 us -> none  [far_term(): chosen = jnp.take(coeff_table, couple_list[0, tree_level], axis=0)]
    ppermute x20 -> x30, starting transfers between devices: 36.5 us -> 33.6 us  [swap(): return lax.ppermute(value, 'leaf', pairs)]
    slice x3 -> x0, local copies, waits for them, and re-layouts: 2.13 us -> none  [the longest x2 1.25 us: apply_slots(): relative[slot_index]]
    ppermute x20 -> x30, waiting for transfers between devices: 16.1 us -> 18.1 us  [swap(): return lax.ppermute(value, 'leaf', pairs)]
  transfers between devices with their start and end apart: 20 -> 30, of which waited for: 4 -> 9; matrix products, arithmetic and copies ran while one was open for 6% -> 1% of each run, Pallas kernels for 0% -> 11%
where the time goes in v1:
time: 75.8 us; the launch traced here: 75.4 us
  starting transfers between devices  33.6 us (44%)
  waiting for transfers between devices  18.1 us (24%)
  Pallas kernels  13.5 us (18%)
  local copies, waits for them, and re-layouts  9.2 us (12%)
  between operations  0.89 us (1%)
    ppermute x30, starting transfers between devices, swap(): return lax.ppermute(value, 'leaf', pairs)  33.6 us
    ppermute x30, waiting for transfers between devices, swap(): return lax.ppermute(value, 'leaf', pairs)  18.1 us
    pallas_call x8, Pallas kernels, call(): pl.pallas_call(kernel, out_shape=out_shape, in_specs=[SM] * ints + [VM] *...  13.5 us
    unnamed x29, local copies, waits for them, and re-layouts  9.2 us
  transfers between devices with their start and end apart: 30, of which 9 were waited for; matrix products, arithmetic and copies ran while one was open for 1% of the time, Pallas kernels for 11%

profile of v1, /device:TPU:0, one launch (start us, length us, event | category | flops | bytes accessed | tf_op | source)
XLA Modules:
  0.0 75.4 jit_solution(10793883477611802704)
XLA Ops:
  0.6 0.6 collective-permute-start.2
  1.2 4.0 %collective-permute-start.1 = (bf16[64,1024]{1,0:T(8,128)(2,1)}, bf16[64,1024]{1,0:T(8,128)(2,1)S(1)}, u32[]{:S(2)}, u32[]{:S(2)}) collective-permute-start(bf16[64,1024]{1,0:T(8,128)(2,1)} %refs_5_.3), channel_id=1, source_target_pairs={{0,2},{1,3},{2,0},{3,1},{4,6},{5,7},{6,4},{7,5},{8,10},{9,11},{10,... | collective-permute-start | bytes 393224 | tf_op jit(solution)/shard_map/ppermute | solution.py:18
  5.2 5.2 %collective-permute-done.1.refs_2_ = bf16[64,1024]{1,0:T(8,128)(2,1)S(1)} collective-permute-done((bf16[64,1024]{1,0:T(8,128)(2,1)}, bf16[64,1024]{1,0:T(8,128)(2,1)S(1)}, u32[]{:S(2)}, u32[]{:S(2)}) %collective-permute-start.1) | collective-permute-done | bytes 131104 | tf_op jit(solution)/shard_map/ppermute | solution.py:18
  10.5 0.1 collective-permute-start.3
  10.6 1.3 %collective-permute-done.3.refs_4_ = bf16[64,1024]{1,0:T(8,128)(2,1)S(1)} collective-permute-done((bf16[64,1024]{1,0:T(8,128)(2,1)S(1)}, bf16[64,1024]{1,0:T(8,128)(2,1)S(1)}, u32[]{:S(2)}, u32[]{:S(2)}) %collective-permute-start.3) | collective-permute-done | bytes 131104 | tf_op jit(solution)/shard_map/ppermute | solution.py:18
  11.9 2.2 %copy-done.1 = bf16[1,2,1024,1024]{3,2,1,0:T(8,128)(2,1)S(1)} copy-done((bf16[1,2,1024,1024]{3,2,1,0:T(8,128)(2,1)S(1)}, bf16[1,2,1024,1024]{3,2,1,0:T(8,128)(2,1)}, u32[]{:S(2)}) %copy-start.1) | copy-done | bytes 4194328
  14.1 0.9 %copy-done.3 = bf16[1,1024,128]{2,1,0:T(8,128)(2,1)S(1)} copy-done((bf16[1,1024,128]{2,1,0:T(8,128)(2,1)S(1)}, bf16[1,1024,128]{2,1,0:T(8,128)(2,1)}, u32[]{:S(2)}) %copy-start.3) | copy-done | bytes 262168
  15.1 0.9 %copy-done.7 = bf16[64,1024]{1,0:T(8,128)(2,1)S(1)} copy-done((bf16[64,1024]{1,0:T(8,128)(2,1)S(1)}, bf16[64,1024]{1,0:T(8,128)(2,1)}, u32[]{:S(2)}) %copy-start.7) | copy-done | bytes 131096
  16.0 0.7 copy-done.11
  16.6 1.5 %shard_map.104 = (f32[64,1024]{1,0:T(8,128)S(1)}, bf16[64,1152]{1,0:T(8,128)(2,1)S(1)}, bf16[64,128]{1,0:T(8,128)(2,1)S(1)}) custom-call(s32[1]{0:T(128)} %bitcast.place_ref, s32[1,2]{1,0:T(1,128)S(1)} %copy-done.11, bf16[64,1024]{1,0:T(8,128)(2,1)S(1)} %copy-done.7, bf16[64,1024]{1,0:T(8,128)(2,1)S(1)} %collective-permute-done.refs_1_, ...), custom_call_target="tpu_custom_call" | custom-call | tf_op jit(solution)/shard_map/pallas_call | solution.py:176
  18.2 0.2 collective-permute-start.15
  18.4 3.7 %collective-permute-start.5 = (bf16[64,1152]{1,0:T(8,128)(2,1)S(1)}, bf16[64,1152]{1,0:T(8,128)(2,1)S(1)}, u32[]{:S(2)}, u32[]{:S(2)}) collective-permute-start(bf16[64,1152]{1,0:T(8,128)(2,1)S(1)} %get-tuple-element.11.refs_0_), channel_id=1, source_target_pairs={{0,2},{1,3},{2,0},{3,1},{4,6},{5,7},{6,4},{7,5},{8,10},{9,11},{10,... | collective-permute-start | bytes 442376 | tf_op jit(solution)/shard_map/ppermute | solution.py:18
  22.1 0.7 copy.12.list_ref
  22.8 1.0 %copy-done.5 = bf16[1,3,4,128,128]{4,3,2,1,0:T(8,128)(2,1)S(1)} copy-done((bf16[1,3,4,128,128]{4,3,2,1,0:T(8,128)(2,1)S(1)}, bf16[1,3,4,128,128]{4,3,2,1,0:T(8,128)(2,1)}, u32[]{:S(2)}) %copy-start.5) | copy-done | bytes 393240
  23.8 0.7 shard_map.105
  24.5 0.6 collective-permute-start.12
  25.1 0.2 collective-permute-start.10
  25.3 2.3 %collective-permute-start.8 = (bf16[2,64,128]{2,1,0:T(8,128)(2,1)S(1)}, bf16[2,64,128]{2,1,0:T(8,128)(2,1)S(1)}, u32[]{:S(2)}, u32[]{:S(2)}) collective-permute-start(bf16[2,64,128]{2,1,0:T(8,128)(2,1)S(1)} %pad_maximum_fusion.2.refs_0_), channel_id=1, source_target_pairs={{0,4},{1,7},{2,6},{3,5},{4,0},{5,3},{6,2},{7,1},{8,12},{9,15},{10,... | collective-permute-start | bytes 98312 | tf_op jit(solution)/shard_map/ppermute | solution.py:18
  27.6 0.6 collective-permute-done.5.refs_2_
  28.2 3.6 %collective-permute-start.7 = (bf16[2,64,128]{2,1,0:T(8,128)(2,1)S(1)}, bf16[2,64,128]{2,1,0:T(8,128)(2,1)S(1)}, u32[]{:S(2)}, u32[]{:S(2)}) collective-permute-start(bf16[2,64,128]{2,1,0:T(8,128)(2,1)S(1)} %pad_maximum_fusion.2.refs_0_), channel_id=1, source_target_pairs={{0,8},{1,11},{2,10},{3,9},{4,12},{5,15},{6,14},{7,13},{8,0},{9,3},... | collective-permute-start | bytes 98312 | tf_op jit(solution)/shard_map/ppermute | solution.py:18
  31.8 4.0 %collective-permute-start.6 = (bf16[2,64,128]{2,1,0:T(8,128)(2,1)S(1)}, bf16[2,64,128]{2,1,0:T(8,128)(2,1)S(1)}, u32[]{:S(2)}, u32[]{:S(2)}) collective-permute-start(bf16[2,64,128]{2,1,0:T(8,128)(2,1)S(1)} %pad_maximum_fusion.2.refs_0_), channel_id=1, source_target_pairs={{0,12},{1,15},{2,14},{3,13},{4,8},{5,11},{6,10},{7,9},{8,4},{9,7},... | collective-permute-start | bytes 98312 | tf_op jit(solution)/shard_map/ppermute | solution.py:18
  35.8 0.5 collective-permute-start.14
  36.3 1.6 %collective-permute-done.6 = bf16[2,64,128]{2,1,0:T(8,128)(2,1)S(1)} collective-permute-done((bf16[2,64,128]{2,1,0:T(8,128)(2,1)S(1)}, bf16[2,64,128]{2,1,0:T(8,128)(2,1)S(1)}, u32[]{:S(2)}, u32[]{:S(2)}) %collective-permute-start.6) | collective-permute-done | bytes 32800 | tf_op jit(solution)/shard_map/ppermute | solution.py:18
  38.0 0.6 collective-permute-start.9
  38.6 1.0 %copy-done.6 = bf16[1,3,4,128,128]{4,3,2,1,0:T(8,128)(2,1)S(1)} copy-done((bf16[1,3,4,128,128]{4,3,2,1,0:T(8,128)(2,1)S(1)}, bf16[1,3,4,128,128]{4,3,2,1,0:T(8,128)(2,1)}, u32[]{:S(2)}) %copy-start.6) | copy-done | bytes 393240
  39.5 0.9 %copy-done.10 = bf16[2,2,128,128]{3,2,1,0:T(8,128)(2,1)S(1)} copy-done((bf16[2,2,128,128]{3,2,1,0:T(8,128)(2,1)S(1)}, bf16[2,2,128,128]{3,2,1,0:T(8,128)(2,1)}, u32[]{:S(2)}) %copy-start.10) | copy-done | bytes 131096
  40.5 3.7 %shard_map.106.refs_3_ = bf16[16,128,128]{2,1,0:T(8,128)(2,1)S(1)} custom-call(s32[1]{0:T(128)} %bitcast.place_ref, s32[1,3,4]{2,1,0:T(4,128)S(1)} %copy.12.list_ref, bf16[3,4,128,128]{3,2,1,0:T(8,128)(2,1)S(1)} %bitcast.22, bf16[2,2,128,128]{3,2,1,0:T(8,128)(2,1)S(1)} %copy-done.10, bf16[8,128,128]{2,1,0:T(8,128)(2,1)S(1)} %get-tuple-element.12.pair_a, ...), custom_call_target="tpu_custom_call" | custom-call | tf_op jit(solution)/shard_map/pallas_call | solution.py:176
  44.2 0.9 %copy-done.8 = bf16[64,1024]{1,0:T(8,128)(2,1)S(1)} copy-done((bf16[64,1024]{1,0:T(8,128)(2,1)S(1)}, bf16[64,1024]{1,0:T(8,128)(2,1)}, u32[]{:S(2)}) %copy-start.8) | copy-done | bytes 131096
  45.1 1.8 %shard_map.107.refs_5_ = f32[64,1024]{1,0:T(8,128)S(1)} custom-call(s32[1]{0:T(128)} %bitcast.place_ref, s32[1,3]{1,0:T(1,128)S(1)} %copy-done.13, bf16[64,1152]{1,0:T(8,128)(2,1)S(1)} %get-tuple-element.11.refs_0_, bf16[64,1152]{1,0:T(8,128)(2,1)S(1)} %collective-permute-done.14.refs_1_, bf16[64,1152]{1,0:T(8,128)(2,1)S(1)} %collective-permute-done.5.refs_2_, ...), custom_call_target="tpu_custom_call" | custom-call | tf_op jit(solution)/shard_map/pallas_call | solution.py:176
  46.9 0.6 shard_map.108.refs_0_
  47.5 0.1 collective-permute-start.19
  47.6 2.3 %collective-permute-start.18 = (bf16[64,1024]{1,0:T(8,128)(2,1)S(1)}, bf16[64,1024]{1,0:T(8,128)(2,1)S(1)}, u32[]{:S(2)}, u32[]{:S(2)}) collective-permute-start(bf16[64,1024]{1,0:T(8,128)(2,1)S(1)} %shard_map.108.refs_0_), channel_id=1, source_target_pairs={{0,2},{1,3},{2,0},{3,1},{4,6},{5,7},{6,4},{7,5},{8,10},{9,11},{10,... | collective-permute-start | bytes 393224 | tf_op jit(solution)/shard_map/ppermute | solution.py:18
  49.8 5.5 %collective-permute-done.18.refs_2_ = bf16[64,1024]{1,0:T(8,128)(2,1)S(1)} collective-permute-done((bf16[64,1024]{1,0:T(8,128)(2,1)S(1)}, bf16[64,1024]{1,0:T(8,128)(2,1)S(1)}, u32[]{:S(2)}, u32[]{:S(2)}) %collective-permute-start.18) | collective-permute-done | bytes 131104 | tf_op jit(solution)/shard_map/ppermute | solution.py:18
  55.4 1.3 %collective-permute-done.20.refs_4_ = bf16[64,1024]{1,0:T(8,128)(2,1)S(1)} collective-permute-done((bf16[64,1024]{1,0:T(8,128)(2,1)S(1)}, bf16[64,1024]{1,0:T(8,128)(2,1)S(1)}, u32[]{:S(2)}, u32[]{:S(2)}) %collective-permute-start.20) | collective-permute-done | bytes 131104 | tf_op jit(solution)/shard_map/ppermute | solution.py:18
  56.7 2.1 %shard_map.109 = (f32[64,1024]{1,0:T(8,128)}, bf16[64,1152]{1,0:T(8,128)(2,1)S(1)}, bf16[64,128]{1,0:T(8,128)(2,1)S(1)}) custom-call(s32[1]{0:T(128)} %bitcast.place_ref, s32[1,2]{1,0:T(1,128)S(1)} %copy-done.12, bf16[64,1024]{1,0:T(8,128)(2,1)S(1)} %shard_map.108.refs_0_, bf16[64,1024]{1,0:T(8,128)(2,1)S(1)} %collective-permute-done.17.refs_1_, ...), custom_call_target="tpu_custom_call" | custom-call | tf_op jit(solution)/shard_map/pallas_call | solution.py:176
  58.9 0.1 collective-permute-start.28
  59.0 3.5 %collective-permute-start.22 = (bf16[64,1152]{1,0:T(8,128)(2,1)S(1)}, bf16[64,1152]{1,0:T(8,128)(2,1)S(1)}, u32[]{:S(2)}, u32[]{:S(2)}) collective-permute-start(bf16[64,1152]{1,0:T(8,128)(2,1)S(1)} %get-tuple-element.17.refs_0_), channel_id=1, source_target_pairs={{0,2},{1,3},{2,0},{3,1},{4,6},{5,7},{6,4},{7,5},{8,10},{9,11},{10,... | collective-permute-start | bytes 442376 | tf_op jit(solution)/shard_map/ppermute | solution.py:18
  62.6 0.5 collective-permute-start.27
  63.1 0.7 collective-permute-done.21
  63.7 1.2 %collective-permute-start.25 = (bf16[2,64,128]{2,1,0:T(8,128)(2,1)S(1)}, bf16[2,64,128]{2,1,0:T(8,128)(2,1)S(1)}, u32[]{:S(2)}, u32[]{:S(2)}) collective-permute-start(bf16[2,64,128]{2,1,0:T(8,128)(2,1)S(1)} %pad_maximum_fusion.3.refs_0_), channel_id=1, source_target_pairs={{0,4},{1,7},{2,6},{3,5},{4,0},{5,3},{6,2},{7,1},{8,12},{9,15},{10,... | collective-permute-start | bytes 98312 | tf_op jit(solution)/shard_map/ppermute | solution.py:18
  64.9 1.4 %collective-permute-start.24 = (bf16[2,64,128]{2,1,0:T(8,128)(2,1)S(1)}, bf16[2,64,128]{2,1,0:T(8,128)(2,1)S(1)}, u32[]{:S(2)}, u32[]{:S(2)}) collective-permute-start(bf16[2,64,128]{2,1,0:T(8,128)(2,1)S(1)} %pad_maximum_fusion.3.refs_0_), channel_id=1, source_target_pairs={{0,8},{1,11},{2,10},{3,9},{4,12},{5,15},{6,14},{7,13},{8,0},{9,3},... | collective-permute-start | bytes 98312 | tf_op jit(solution)/shard_map/ppermute | solution.py:18
  66.3 4.0 %collective-permute-start.23 = (bf16[2,64,128]{2,1,0:T(8,128)(2,1)S(1)}, bf16[2,64,128]{2,1,0:T(8,128)(2,1)S(1)}, u32[]{:S(2)}, u32[]{:S(2)}) collective-permute-start(bf16[2,64,128]{2,1,0:T(8,128)(2,1)S(1)} %pad_maximum_fusion.3.refs_0_), channel_id=1, source_target_pairs={{0,12},{1,15},{2,14},{3,13},{4,8},{5,11},{6,10},{7,9},{8,4},{9,7},... | collective-permute-start | bytes 98312 | tf_op jit(solution)/shard_map/ppermute | solution.py:18
  70.3 0.1 collective-permute-start.29
  70.4 0.3 collective-permute-done.24
  70.7 1.5 %collective-permute-done.23 = bf16[2,64,128]{2,1,0:T(8,128)(2,1)S(1)} collective-permute-done((bf16[2,64,128]{2,1,0:T(8,128)(2,1)S(1)}, bf16[2,64,128]{2,1,0:T(8,128)(2,1)S(1)}, u32[]{:S(2)}, u32[]{:S(2)}) %collective-permute-start.23) | collective-permute-done | bytes 32800 | tf_op jit(solution)/shard_map/ppermute | solution.py:18
  72.2 0.1 collective-permute-start.26
  72.3 1.8 %shard_map.110.refs_5_ = f32[64,1024]{1,0:T(8,128)S(1)} custom-call(s32[1]{0:T(128)} %bitcast.place_ref, s32[1,3]{1,0:T(1,128)S(1)} %copy-done.13, bf16[64,1152]{1,0:T(8,128)(2,1)S(1)} %get-tuple-element.17.refs_0_, bf16[64,1152]{1,0:T(8,128)(2,1)S(1)} %collective-permute-done.27.refs_1_, bf16[64,1152]{1,0:T(8,128)(2,1)S(1)} %collective-permute-done.22.refs_2_, ...), custom_call_target="tpu_custom_call" | custom-call | tf_op jit(solution)/shard_map/pallas_call | solution.py:176
  74.1 1.3 %shard_map.111 = f32[64,1024]{1,0:T(8,128)} custom-call(s32[1]{0:T(128)} %bitcast.place_ref, bf16[2,64,128]{2,1,0:T(8,128)(2,1)S(1)} %pad_maximum_fusion.3.refs_0_, bf16[7,64,128]{2,1,0:T(8,128)(2,1)S(1)} %pad_maximum_fusion.1.refs_1_, bf16[7,64,128]{2,1,0:T(8,128)(2,1)S(1)} %collective-permute-done.26.refs_2_, ...), custom_call_target="tpu_custom_call" | custom-call | tf_op jit(solution)/shard_map/pallas_call | solution.py:176
  (59 shorter events, 0.3 us)
Async XLA Ops:
  0.6 43.5 %copy-start.13 = (s32[1,3]{1,0:T(1,128)S(1)}, s32[1,3]{1,0:T(1,128)}, u32[]{:S(2)}) copy-start(s32[1,3]{1,0:T(1,128)} %list_ref.9) | copy-start | bytes 40
  0.6 4.6 %collective-permute-start.2 = (bf16[64,1024]{1,0:T(8,128)(2,1)}, bf16[64,1024]{1,0:T(8,128)(2,1)S(1)}, u32[]{:S(2)}, u32[]{:S(2)}) collective-permute-start(bf16[64,1024]{1,0:T(8,128)(2,1)} %refs_5_.3), channel_id=1, source_target_pairs={{2,4},{3,5},{4,2},{5,3},{6,8},{7,9},{8,6},{9,7},{10,12},{11,13},{1... | collective-permute-start | bytes 393224 | tf_op jit(solution)/shard_map/ppermute | solution.py:18
  1.2 9.3 %collective-permute-start.1 = (bf16[64,1024]{1,0:T(8,128)(2,1)}, bf16[64,1024]{1,0:T(8,128)(2,1)S(1)}, u32[]{:S(2)}, u32[]{:S(2)}) collective-permute-start(bf16[64,1024]{1,0:T(8,128)(2,1)} %refs_5_.3), channel_id=1, source_target_pairs={{0,2},{1,3},{2,0},{3,1},{4,6},{5,7},{6,4},{7,5},{8,10},{9,11},{10,... | collective-permute-start | bytes 393224 | tf_op jit(solution)/shard_map/ppermute | solution.py:18
  5.2 5.4 %collective-permute-start = (bf16[64,1024]{1,0:T(8,128)(2,1)}, bf16[64,1024]{1,0:T(8,128)(2,1)S(1)}, u32[]{:S(2)}, u32[]{:S(2)}) collective-permute-start(bf16[64,1024]{1,0:T(8,128)(2,1)} %refs_5_.3), channel_id=1, source_target_pairs={{0,1},{1,0},{2,3},{3,2},{4,5},{5,4},{6,7},{7,6},{8,9},{9,8},{10,11... | collective-permute-start | bytes 393224 | tf_op jit(solution)/shard_map/ppermute | solution.py:18
  5.2 51.5 %copy-start.12 = (s32[1,2]{1,0:T(1,128)S(1)}, s32[1,2]{1,0:T(1,128)}, u32[]{:S(2)}) copy-start(s32[1,2]{1,0:T(1,128)} %list_ref.8) | copy-start | bytes 28
  5.2 39.0 %copy-start = (bf16[1,3,1024,1024]{3,2,1,0:T(8,128)(2,1)S(1)}, bf16[1,3,1024,1024]{3,2,1,0:T(8,128)(2,1)}, u32[]{:S(2)}) copy-start(bf16[1,3,1024,1024]{3,2,1,0:T(8,128)(2,1)} %param.11) | copy-start | bytes 18874372
  10.5 1.4 %collective-permute-start.3 = (bf16[64,1024]{1,0:T(8,128)(2,1)S(1)}, bf16[64,1024]{1,0:T(8,128)(2,1)S(1)}, u32[]{:S(2)}, u32[]{:S(2)}) collective-permute-start(bf16[64,1024]{1,0:T(8,128)(2,1)S(1)} %broadcast_select_fusion.3), channel_id=1, source_target_pairs={{0,1},{1,0},{2,3},{3,2},{4,5},{5,4},{6,7},{7,6},{8,9},{9,8},{10,11... | collective-permute-start | bytes 393224 | tf_op jit(solution)/shard_map/ppermute | solution.py:18
  11.9 2.2 %copy-start.1 = (bf16[1,2,1024,1024]{3,2,1,0:T(8,128)(2,1)S(1)}, bf16[1,2,1024,1024]{3,2,1,0:T(8,128)(2,1)}, u32[]{:S(2)}) copy-start(bf16[1,2,1024,1024]{3,2,1,0:T(8,128)(2,1)} %param.13) | copy-start | bytes 12582916
  14.1 0.9 %copy-start.3 = (bf16[1,1024,128]{2,1,0:T(8,128)(2,1)S(1)}, bf16[1,1024,128]{2,1,0:T(8,128)(2,1)}, u32[]{:S(2)}) copy-start(bf16[1,1024,128]{2,1,0:T(8,128)(2,1)} %param.14) | copy-start | bytes 786436
  15.1 0.9 %copy-start.7 = (bf16[64,1024]{1,0:T(8,128)(2,1)S(1)}, bf16[64,1024]{1,0:T(8,128)(2,1)}, u32[]{:S(2)}) copy-start(bf16[64,1024]{1,0:T(8,128)(2,1)} %refs_5_.3) | copy-start | bytes 393220
  16.0 0.7 copy-start.11
  18.1 38.6 %copy-start.2 = (bf16[1,2,1024,1024]{3,2,1,0:T(8,128)(2,1)S(1)}, bf16[1,2,1024,1024]{3,2,1,0:T(8,128)(2,1)}, u32[]{:S(2)}) copy-start(bf16[1,2,1024,1024]{3,2,1,0:T(8,128)(2,1)} %param.13) | copy-start | bytes 12582916
  18.2 38.6 %copy-start.4 = (bf16[1,1024,128]{2,1,0:T(8,128)(2,1)S(1)}, bf16[1,1024,128]{2,1,0:T(8,128)(2,1)}, u32[]{:S(2)}) copy-start(bf16[1,1024,128]{2,1,0:T(8,128)(2,1)} %param.14) | copy-start | bytes 786436
  18.2 7.1 %collective-permute-start.15 = (bf16[64,1152]{1,0:T(8,128)(2,1)S(1)}, bf16[64,1152]{1,0:T(8,128)(2,1)S(1)}, u32[]{:S(2)}, u32[]{:S(2)}) collective-permute-start(bf16[64,1152]{1,0:T(8,128)(2,1)S(1)} %get-tuple-element.11.refs_0_), channel_id=1, source_target_pairs={{2,4},{3,5},{4,2},{5,3},{6,8},{7,9},{8,6},{9,7},{10,12},{11,13},{1... | collective-permute-start | bytes 442376 | tf_op jit(solution)/shard_map/ppermute | solution.py:18
  18.4 9.8 %collective-permute-start.5 = (bf16[64,1152]{1,0:T(8,128)(2,1)S(1)}, bf16[64,1152]{1,0:T(8,128)(2,1)S(1)}, u32[]{:S(2)}, u32[]{:S(2)}) collective-permute-start(bf16[64,1152]{1,0:T(8,128)(2,1)S(1)} %get-tuple-element.11.refs_0_), channel_id=1, source_target_pairs={{0,2},{1,3},{2,0},{3,1},{4,6},{5,7},{6,4},{7,5},{8,10},{9,11},{10,... | collective-permute-start | bytes 442376 | tf_op jit(solution)/shard_map/ppermute | solution.py:18
  22.1 3.0 %collective-permute-start.4 = (bf16[64,128]{1,0:T(8,128)(2,1)S(1)}, bf16[64,128]{1,0:T(8,128)(2,1)S(1)}, u32[]{:S(2)}, u32[]{:S(2)}) collective-permute-start(bf16[64,128]{1,0:T(8,128)(2,1)S(1)} %get-tuple-element.10), channel_id=1, source_target_pairs={{0,1},{1,0},{2,3},{3,2},{4,5},{5,4},{6,7},{7,6},{8,9},{9,8},{10,11... | collective-permute-start | bytes 49160 | tf_op jit(solution)/shard_map/ppermute | solution.py:18
  22.8 1.0 %copy-start.5 = (bf16[1,3,4,128,128]{4,3,2,1,0:T(8,128)(2,1)S(1)}, bf16[1,3,4,128,128]{4,3,2,1,0:T(8,128)(2,1)}, u32[]{:S(2)}) copy-start(bf16[1,3,4,128,128]{4,3,2,1,0:T(8,128)(2,1)} %param.17) | copy-start | bytes 1179652
  24.5 13.4 %collective-permute-start.12 = (bf16[4,128,128]{2,1,0:T(8,128)(2,1)S(1)}, bf16[4,128,128]{2,1,0:T(8,128)(2,1)S(1)}, u32[]{:S(2)}, u32[]{:S(2)}) collective-permute-start(bf16[4,128,128]{2,1,0:T(8,128)(2,1)S(1)} %get-tuple-element.13.qa), channel_id=1, source_target_pairs={{0,1},{1,0},{2,3},{3,2},{4,5},{5,4},{6,7},{7,6},{8,9},{9,8},{10,11... | collective-permute-start | bytes 393224 | tf_op jit(solution)/shard_map/ppermute | solution.py:18
  25.1 6.7 %collective-permute-start.11 = (bf16[4,128,128]{2,1,0:T(8,128)(2,1)S(1)}, bf16[4,128,128]{2,1,0:T(8,128)(2,1)S(1)}, u32[]{:S(2)}, u32[]{:S(2)}) collective-permute-start(bf16[4,128,128]{2,1,0:T(8,128)(2,1)S(1)} %get-tuple-element.13.qa), channel_id=1, source_target_pairs={{0,2},{1,3},{2,0},{3,1},{4,6},{5,7},{6,4},{7,5},{8,10},{9,11},{10,... | collective-permute-start | bytes 393224 | tf_op jit(solution)/shard_map/ppermute | solution.py:18
  25.1 13.4 %collective-permute-start.10 = (bf16[8,128,128]{2,1,0:T(8,128)(2,1)S(1)}, bf16[8,128,128]{2,1,0:T(8,128)(2,1)S(1)}, u32[]{:S(2)}, u32[]{:S(2)}) collective-permute-start(bf16[8,128,128]{2,1,0:T(8,128)(2,1)S(1)} %get-tuple-element.12.pair_a), channel_id=1, source_target_pairs={{0,1},{1,0},{2,3},{3,2},{4,5},{5,4},{6,7},{7,6},{8,9},{9,8},{10,11... | collective-permute-start | bytes 786440 | tf_op jit(solution)/shard_map/ppermute | solution.py:18
  25.3 10.5 %collective-permute-start.8 = (bf16[2,64,128]{2,1,0:T(8,128)(2,1)S(1)}, bf16[2,64,128]{2,1,0:T(8,128)(2,1)S(1)}, u32[]{:S(2)}, u32[]{:S(2)}) collective-permute-start(bf16[2,64,128]{2,1,0:T(8,128)(2,1)S(1)} %pad_maximum_fusion.2.refs_0_), channel_id=1, source_target_pairs={{0,4},{1,7},{2,6},{3,5},{4,0},{5,3},{6,2},{7,1},{8,12},{9,15},{10,... | collective-permute-start | bytes 98312 | tf_op jit(solution)/shard_map/ppermute | solution.py:18
  28.2 7.6 %collective-permute-start.7 = (bf16[2,64,128]{2,1,0:T(8,128)(2,1)S(1)}, bf16[2,64,128]{2,1,0:T(8,128)(2,1)S(1)}, u32[]{:S(2)}, u32[]{:S(2)}) collective-permute-start(bf16[2,64,128]{2,1,0:T(8,128)(2,1)S(1)} %pad_maximum_fusion.2.refs_0_), channel_id=1, source_target_pairs={{0,8},{1,11},{2,10},{3,9},{4,12},{5,15},{6,14},{7,13},{8,0},{9,3},... | collective-permute-start | bytes 98312 | tf_op jit(solution)/shard_map/ppermute | solution.py:18
  31.8 6.2 %collective-permute-start.6 = (bf16[2,64,128]{2,1,0:T(8,128)(2,1)S(1)}, bf16[2,64,128]{2,1,0:T(8,128)(2,1)S(1)}, u32[]{:S(2)}, u32[]{:S(2)}) collective-permute-start(bf16[2,64,128]{2,1,0:T(8,128)(2,1)S(1)} %pad_maximum_fusion.2.refs_0_), channel_id=1, source_target_pairs={{0,12},{1,15},{2,14},{3,13},{4,8},{5,11},{6,10},{7,9},{8,4},{9,7},... | collective-permute-start | bytes 98312 | tf_op jit(solution)/shard_map/ppermute | solution.py:18
  35.8 2.7 %collective-permute-start.13 = (bf16[4,128,128]{2,1,0:T(8,128)(2,1)S(1)}, bf16[4,128,128]{2,1,0:T(8,128)(2,1)S(1)}, u32[]{:S(2)}, u32[]{:S(2)}) collective-permute-start(bf16[4,128,128]{2,1,0:T(8,128)(2,1)S(1)} %collective-permute-done.11.qb), channel_id=1, source_target_pairs={{0,1},{1,0},{2,3},{3,2},{4,5},{5,4},{6,7},{7,6},{8,9},{9,8},{10,11... | collective-permute-start | bytes 393224 | tf_op jit(solution)/shard_map/ppermute | solution.py:18
  35.8 8.3 %collective-permute-start.14 = (bf16[64,1152]{1,0:T(8,128)(2,1)S(1)}, bf16[64,1152]{1,0:T(8,128)(2,1)S(1)}, u32[]{:S(2)}, u32[]{:S(2)}) collective-permute-start(bf16[64,1152]{1,0:T(8,128)(2,1)S(1)} %get-tuple-element.11.refs_0_), channel_id=1, source_target_pairs={{0,1},{1,0},{2,3},{3,2},{4,5},{5,4},{6,7},{7,6},{8,9},{9,8},{10,11... | collective-permute-start | bytes 442376 | tf_op jit(solution)/shard_map/ppermute | solution.py:18
  37.9 6.2 %collective-permute-start.16 = (bf16[64,1152]{1,0:T(8,128)(2,1)S(1)}, bf16[64,1152]{1,0:T(8,128)(2,1)S(1)}, u32[]{:S(2)}, u32[]{:S(2)}) collective-permute-start(bf16[64,1152]{1,0:T(8,128)(2,1)S(1)} %broadcast_select_fusion.1), channel_id=1, source_target_pairs={{0,1},{1,0},{2,3},{3,2},{4,5},{5,4},{6,7},{7,6},{8,9},{9,8},{10,11... | collective-permute-start | bytes 442376 | tf_op jit(solution)/shard_map/ppermute | solution.py:18
  38.0 8.9 %collective-permute-start.9 = (bf16[7,64,128]{2,1,0:T(8,128)(2,1)S(1)}, bf16[7,64,128]{2,1,0:T(8,128)(2,1)S(1)}, u32[]{:S(2)}, u32[]{:S(2)}) collective-permute-start(bf16[7,64,128]{2,1,0:T(8,128)(2,1)S(1)} %pad_maximum_fusion.refs_1_), channel_id=1, source_target_pairs={{0,1},{1,0},{2,3},{3,2},{4,5},{5,4},{6,7},{7,6},{8,9},{9,8},{10,11... | collective-permute-start | bytes 344072 | tf_op jit(solution)/shard_map/ppermute | solution.py:18
  38.5 1.0 %copy-start.6 = (bf16[1,3,4,128,128]{4,3,2,1,0:T(8,128)(2,1)S(1)}, bf16[1,3,4,128,128]{4,3,2,1,0:T(8,128)(2,1)}, u32[]{:S(2)}) copy-start(bf16[1,3,4,128,128]{4,3,2,1,0:T(8,128)(2,1)} %param.17) | copy-start | bytes 1179652
  39.5 0.9 %copy-start.10 = (bf16[2,2,128,128]{3,2,1,0:T(8,128)(2,1)S(1)}, bf16[2,2,128,128]{3,2,1,0:T(8,128)(2,1)}, u32[]{:S(2)}) copy-start(bf16[2,2,128,128]{3,2,1,0:T(8,128)(2,1)} %maps.1) | copy-start | bytes 393220
  44.2 0.9 %copy-start.8 = (bf16[64,1024]{1,0:T(8,128)(2,1)S(1)}, bf16[64,1024]{1,0:T(8,128)(2,1)}, u32[]{:S(2)}) copy-start(bf16[64,1024]{1,0:T(8,128)(2,1)} %refs_5_.3) | copy-start | bytes 393220
  45.1 27.2 %copy-start.9 = (bf16[64,1024]{1,0:T(8,128)(2,1)S(1)}, bf16[64,1024]{1,0:T(8,128)(2,1)}, u32[]{:S(2)}) copy-start(bf16[64,1024]{1,0:T(8,128)(2,1)} %refs_5_.3) | copy-start | bytes 393220
  47.5 2.4 %collective-permute-start.19 = (bf16[64,1024]{1,0:T(8,128)(2,1)S(1)}, bf16[64,1024]{1,0:T(8,128)(2,1)S(1)}, u32[]{:S(2)}, u32[]{:S(2)}) collective-permute-start(bf16[64,1024]{1,0:T(8,128)(2,1)S(1)} %shard_map.108.refs_0_), channel_id=1, source_target_pairs={{2,4},{3,5},{4,2},{5,3},{6,8},{7,9},{8,6},{9,7},{10,12},{11,13},{1... | collective-permute-start | bytes 393224 | tf_op jit(solution)/shard_map/ppermute | solution.py:18
  47.6 7.7 %collective-permute-start.18 = (bf16[64,1024]{1,0:T(8,128)(2,1)S(1)}, bf16[64,1024]{1,0:T(8,128)(2,1)S(1)}, u32[]{:S(2)}, u32[]{:S(2)}) collective-permute-start(bf16[64,1024]{1,0:T(8,128)(2,1)S(1)} %shard_map.108.refs_0_), channel_id=1, source_target_pairs={{0,2},{1,3},{2,0},{3,1},{4,6},{5,7},{6,4},{7,5},{8,10},{9,11},{10,... | collective-permute-start | bytes 393224 | tf_op jit(solution)/shard_map/ppermute | solution.py:18
  49.8 5.6 %collective-permute-start.17 = (bf16[64,1024]{1,0:T(8,128)(2,1)S(1)}, bf16[64,1024]{1,0:T(8,128)(2,1)S(1)}, u32[]{:S(2)}, u32[]{:S(2)}) collective-permute-start(bf16[64,1024]{1,0:T(8,128)(2,1)S(1)} %shard_map.108.refs_0_), channel_id=1, source_target_pairs={{0,1},{1,0},{2,3},{3,2},{4,5},{5,4},{6,7},{7,6},{8,9},{9,8},{10,11... | collective-permute-start | bytes 393224 | tf_op jit(solution)/shard_map/ppermute | solution.py:18
  55.3 1.4 %collective-permute-start.20 = (bf16[64,1024]{1,0:T(8,128)(2,1)S(1)}, bf16[64,1024]{1,0:T(8,128)(2,1)S(1)}, u32[]{:S(2)}, u32[]{:S(2)}) collective-permute-start(bf16[64,1024]{1,0:T(8,128)(2,1)S(1)} %broadcast_select_fusion.2), channel_id=1, source_target_pairs={{0,1},{1,0},{2,3},{3,2},{4,5},{5,4},{6,7},{7,6},{8,9},{9,8},{10,11... | collective-permute-start | bytes 393224 | tf_op jit(solution)/shard_map/ppermute | solution.py:18
  58.9 7.4 %collective-permute-start.28 = (bf16[64,1152]{1,0:T(8,128)(2,1)S(1)}, bf16[64,1152]{1,0:T(8,128)(2,1)S(1)}, u32[]{:S(2)}, u32[]{:S(2)}) collective-permute-start(bf16[64,1152]{1,0:T(8,128)(2,1)S(1)} %get-tuple-element.17.refs_0_), channel_id=1, source_target_pairs={{2,4},{3,5},{4,2},{5,3},{6,8},{7,9},{8,6},{9,7},{10,12},{11,13},{1... | collective-permute-start | bytes 442376 | tf_op jit(solution)/shard_map/ppermute | solution.py:18
  59.0 11.3 %collective-permute-start.22 = (bf16[64,1152]{1,0:T(8,128)(2,1)S(1)}, bf16[64,1152]{1,0:T(8,128)(2,1)S(1)}, u32[]{:S(2)}, u32[]{:S(2)}) collective-permute-start(bf16[64,1152]{1,0:T(8,128)(2,1)S(1)} %get-tuple-element.17.refs_0_), channel_id=1, source_target_pairs={{0,2},{1,3},{2,0},{3,1},{4,6},{5,7},{6,4},{7,5},{8,10},{9,11},{10,... | collective-permute-start | bytes 442376 | tf_op jit(solution)/shard_map/ppermute | solution.py:18
  62.6 1.2 %collective-permute-start.21 = (bf16[64,128]{1,0:T(8,128)(2,1)S(1)}, bf16[64,128]{1,0:T(8,128)(2,1)S(1)}, u32[]{:S(2)}, u32[]{:S(2)}) collective-permute-start(bf16[64,128]{1,0:T(8,128)(2,1)S(1)} %get-tuple-element.16), channel_id=1, source_target_pairs={{0,1},{1,0},{2,3},{3,2},{4,5},{5,4},{6,7},{7,6},{8,9},{9,8},{10,11... | collective-permute-start | bytes 49160 | tf_op jit(solution)/shard_map/ppermute | solution.py:18
  62.6 9.7 %collective-permute-start.27 = (bf16[64,1152]{1,0:T(8,128)(2,1)S(1)}, bf16[64,1152]{1,0:T(8,128)(2,1)S(1)}, u32[]{:S(2)}, u32[]{:S(2)}) collective-permute-start(bf16[64,1152]{1,0:T(8,128)(2,1)S(1)} %get-tuple-element.17.refs_0_), channel_id=1, source_target_pairs={{0,1},{1,0},{2,3},{3,2},{4,5},{5,4},{6,7},{7,6},{8,9},{9,8},{10,11... | collective-permute-start | bytes 442376 | tf_op jit(solution)/shard_map/ppermute | solution.py:18
  63.7 6.7 %collective-permute-start.25 = (bf16[2,64,128]{2,1,0:T(8,128)(2,1)S(1)}, bf16[2,64,128]{2,1,0:T(8,128)(2,1)S(1)}, u32[]{:S(2)}, u32[]{:S(2)}) collective-permute-start(bf16[2,64,128]{2,1,0:T(8,128)(2,1)S(1)} %pad_maximum_fusion.3.refs_0_), channel_id=1, source_target_pairs={{0,4},{1,7},{2,6},{3,5},{4,0},{5,3},{6,2},{7,1},{8,12},{9,15},{10,... | collective-permute-start | bytes 98312 | tf_op jit(solution)/shard_map/ppermute | solution.py:18
  64.9 5.8 %collective-permute-start.24 = (bf16[2,64,128]{2,1,0:T(8,128)(2,1)S(1)}, bf16[2,64,128]{2,1,0:T(8,128)(2,1)S(1)}, u32[]{:S(2)}, u32[]{:S(2)}) collective-permute-start(bf16[2,64,128]{2,1,0:T(8,128)(2,1)S(1)} %pad_maximum_fusion.3.refs_0_), channel_id=1, source_target_pairs={{0,8},{1,11},{2,10},{3,9},{4,12},{5,15},{6,14},{7,13},{8,0},{9,3},... | collective-permute-start | bytes 98312 | tf_op jit(solution)/shard_map/ppermute | solution.py:18
  66.3 5.8 %collective-permute-start.23 = (bf16[2,64,128]{2,1,0:T(8,128)(2,1)S(1)}, bf16[2,64,128]{2,1,0:T(8,128)(2,1)S(1)}, u32[]{:S(2)}, u32[]{:S(2)}) collective-permute-start(bf16[2,64,128]{2,1,0:T(8,128)(2,1)S(1)} %pad_maximum_fusion.3.refs_0_), channel_id=1, source_target_pairs={{0,12},{1,15},{2,14},{3,13},{4,8},{5,11},{6,10},{7,9},{8,4},{9,7},... | collective-permute-start | bytes 98312 | tf_op jit(solution)/shard_map/ppermute | solution.py:18
  70.3 2.0 %collective-permute-start.29 = (bf16[64,1152]{1,0:T(8,128)(2,1)S(1)}, bf16[64,1152]{1,0:T(8,128)(2,1)S(1)}, u32[]{:S(2)}, u32[]{:S(2)}) collective-permute-start(bf16[64,1152]{1,0:T(8,128)(2,1)S(1)} %broadcast_select_fusion), channel_id=1, source_target_pairs={{0,1},{1,0},{2,3},{3,2},{4,5},{5,4},{6,7},{7,6},{8,9},{9,8},{10,11... | collective-permute-start | bytes 442376 | tf_op jit(solution)/shard_map/ppermute | solution.py:18
  72.2 1.9 %collective-permute-start.26 = (bf16[7,64,128]{2,1,0:T(8,128)(2,1)S(1)}, bf16[7,64,128]{2,1,0:T(8,128)(2,1)S(1)}, u32[]{:S(2)}, u32[]{:S(2)}) collective-permute-start(bf16[7,64,128]{2,1,0:T(8,128)(2,1)S(1)} %pad_maximum_fusion.1.refs_1_), channel_id=1, source_target_pairs={{0,1},{1,0},{2,3},{3,2},{4,5},{5,4},{6,7},{7,6},{8,9},{9,8},{10,11... | collective-permute-start | bytes 344072 | tf_op jit(solution)/shard_map/ppermute | solution.py:18
